TPU v7x, 256 devices: a whole 4x4x8 slice. The times are simulated.
256 devices in a mesh: expert: 64 (over x, z, core), dp: 4 (over y).
Axes of the slice: x: 4, y: 4, z: 8, core: 2. Of those that a mesh axis runs over, the one named last changes fastest.
Arguments:
- tokens: bfloat16 [8192, 3584], P('expert', 'dp'), may hold values from -6 to 6
- cotangent: bfloat16 [8192, 3584], P('expert', 'dp'), may hold values from -6 to 6
- expert_ids: int32 [8192, 8], P('expert'), may hold values from 0 to 63, all different within a row; in each aligned block of 128 rows (0 to 127, 128 to 255, ...) at most 18 rows name the same one
- gate_units: int32 [8192, 8], P('expert'), may hold values from 1 to 255
- w_in: bfloat16 [64, 3584, 1024], P('expert', 'dp'), may hold values from -0.09375 to 0.09375
- w_out: bfloat16 [64, 1024, 3584], P('expert', None, 'dp'), may hold values from -0.1875 to 0.1875
- shared_in: bfloat16 [3584, 1024], P('dp', 'expert'), may hold values from -0.09375 to 0.09375
- shared_out: bfloat16 [1024, 3584], P('expert', 'dp'), may hold values from -0.1875 to 0.1875
Outputs:
- mixed_out: bfloat16 [8192, 3584], P('expert', 'dp')
- input_grad: bfloat16 [8192, 3584], P('expert', 'dp')
- grad_w_in: bfloat16 [64, 3584, 1024], P('expert', 'dp')
- grad_w_out: bfloat16 [64, 1024, 3584], P('expert', None, 'dp')
- grad_shared_in: bfloat16 [3584, 1024], P('dp', 'expert')
- grad_shared_out: bfloat16 [1024, 3584], P('expert', 'dp')
Inputs may be any that keep to these rules, and one draw needn't show every extreme that they name: `expert_ids`: each row names 8 different experts. In each aligned block of 128 rows (the tokens of one index of expert) no expert is named by more than 18 rows, a bound that some block reaches.
All inputs are finite; a program needn't handle non-finite values.
Results may differ from a plain program's by a relative error of at most 0.02.
Values may be sent and summed in bfloat16 or wider, within the bound.
No kernel may reach another device: no remote copies, remote signals or barrier semaphores. Data moves between devices by JAX's collectives and lax.ppermute only.
A program may use at most 128 MiB of HBM per device.

v0:
```python
import jax
import jax.numpy as jnp
from jax import lax
from jax.sharding import PartitionSpec as P


def silu_slope(inputs):
    logistic = jax.nn.sigmoid(inputs)
    return logistic * (1.0 + inputs * (1.0 - logistic))


def contract(first_op, second_op, first_axis, second_axis):
    return lax.dot_general(
        first_op,
        second_op,
        (((first_axis,), (second_axis,)), ((), ())),
        preferred_element_type=jnp.float32,
    )


def local(tokens, cotangent, expert_ids, gate_units, w_in, w_out, shared_in, shared_out):
    experts = lax.axis_size("expert")
    tok_rows, features = tokens.shape
    per_token = expert_ids.shape[1]
    capacity = min(tok_rows, tok_rows * per_token // experts + tok_rows // 64)
    slot_count = experts * capacity
    pair_count = tok_rows * per_token
    flat_ids = expert_ids.reshape(pair_count)
    weights = gate_units.reshape(pair_count).astype(jnp.float32) / 256.0
    one_hot = (flat_ids[:, None] == jnp.arange(experts, dtype=jnp.int32)[None, :]).astype(jnp.int32)
    slot_rank = jnp.sum((jnp.cumsum(one_hot, axis=0) - 1) * one_hot, axis=1)
    target = flat_ids * capacity + slot_rank
    pair_of_slot = (
        jnp.zeros((slot_count,), jnp.int32).at[target].set(jnp.arange(pair_count, dtype=jnp.int32))
    )
    filled = jnp.zeros((slot_count,), jnp.bool_).at[target].set(True)
    token_of_slot = pair_of_slot // per_token
    outgoing = jnp.where(filled[:, None], tokens[token_of_slot], jnp.zeros((), jnp.bfloat16))
    arrived = lax.all_to_all(
        outgoing.reshape(experts, capacity, features),
        "expert",
        split_axis=0,
        concat_axis=0,
        tiled=True,
    ).reshape(slot_count, features)
    full_in, full_out = (
        lax.all_gather(shared_in, "expert", axis=1, tiled=True),
        lax.all_gather(shared_out, "expert", axis=0, tiled=True),
    )
    routed_part = jnp.dot(arrived, w_in[0], preferred_element_type=jnp.float32)
    shared_part = jnp.dot(tokens, full_in, preferred_element_type=jnp.float32)
    pre_act, shared_pre = (
        lax.psum(routed_part.astype(jnp.bfloat16), "dp").astype(jnp.float32),
        lax.psum(shared_part.astype(jnp.bfloat16), "dp").astype(jnp.float32),
    )
    hidden = jax.nn.silu(pre_act).astype(jnp.bfloat16)
    shared_hidden = jax.nn.silu(shared_pre).astype(jnp.bfloat16)
    expert_out = jnp.dot(hidden, w_out[0], preferred_element_type=jnp.float32).astype(jnp.bfloat16)
    returned = lax.all_to_all(
        expert_out.reshape(experts, capacity, features),
        "expert",
        split_axis=0,
        concat_axis=0,
        tiled=True,
    ).reshape(slot_count, features)
    picked = returned[target].astype(jnp.float32) * weights[:, None]
    routed_sum = jnp.sum(picked.reshape(tok_rows, per_token, features), axis=1)
    mixed_out = (
        jnp.dot(shared_hidden, full_out, preferred_element_type=jnp.float32) + routed_sum
    ).astype(jnp.bfloat16)
    scaled = weights[pair_of_slot][:, None] * cotangent[token_of_slot].astype(jnp.float32)
    grad_out = jnp.where(filled[:, None], scaled, jnp.float32(0.0)).astype(jnp.bfloat16)
    grad_rows = lax.all_to_all(
        grad_out.reshape(experts, capacity, features),
        "expert",
        split_axis=0,
        concat_axis=0,
        tiled=True,
    ).reshape(slot_count, features)
    routed_back = contract(grad_rows, w_out[0], 1, 1)
    shared_back = contract(cotangent, full_out, 1, 1)
    hidden_grad, shared_hgrad = (
        lax.psum(routed_back.astype(jnp.bfloat16), "dp").astype(jnp.float32),
        lax.psum(shared_back.astype(jnp.bfloat16), "dp").astype(jnp.float32),
    )
    pre_grad = (hidden_grad * silu_slope(pre_act)).astype(jnp.bfloat16)
    shared_pgrad = (shared_hgrad * silu_slope(shared_pre)).astype(jnp.bfloat16)
    input_rows = contract(pre_grad, w_in[0], 1, 1).astype(jnp.bfloat16)
    sent_back = lax.all_to_all(
        input_rows.reshape(experts, capacity, features),
        "expert",
        split_axis=0,
        concat_axis=0,
        tiled=True,
    ).reshape(slot_count, features)
    routed_dx = jnp.sum(
        sent_back[target].astype(jnp.float32).reshape(tok_rows, per_token, features), axis=1
    )
    input_grad = (contract(shared_pgrad, full_in, 1, 1) + routed_dx).astype(jnp.bfloat16)
    grad_w_in = contract(arrived, pre_grad, 0, 0).astype(jnp.bfloat16)[None]
    grad_w_out = contract(hidden, grad_rows, 0, 0).astype(jnp.bfloat16)[None]
    partial_in = contract(tokens, shared_pgrad, 0, 0)
    partial_out = contract(shared_hidden, cotangent, 0, 0)
    summed_in, summed_out = (
        lax.psum_scatter(partial_in, "expert", scatter_dimension=1, tiled=True),
        lax.psum_scatter(partial_out, "expert", scatter_dimension=0, tiled=True),
    )
    return (
        mixed_out,
        input_grad,
        grad_w_in,
        grad_w_out,
        summed_in.astype(jnp.bfloat16),
        summed_out.astype(jnp.bfloat16),
    )


def solution(mesh):
    return jax.shard_map(
        local,
        mesh=mesh,
        in_specs=(
            P("expert", "dp"),
            P("expert", "dp"),
            P("expert", None),
            P("expert", None),
            P("expert", "dp", None),
            P("expert", None, "dp"),
            P("dp", "expert"),
            P("expert", "dp"),
        ),
        out_specs=(
            P("expert", "dp"),
            P("expert", "dp"),
            P("expert", "dp", None),
            P("expert", None, "dp"),
            P("dp", "expert"),
            P("expert", "dp"),
        ),
        check_vma=False,
    )
```

profile of v0, /device:TPU:8, one launch (start us, length us, event | category | flops | bytes accessed | tf_op | source)
XLA Modules:
  0.0 643.2 jit_solution(7571708094391485513)
XLA Ops:
  9.8 18.0 %reduce-window.6 = s32[64,8,128]{2,1,0:T(8,128)S(1)} reduce-window(s32[64,8,128]{2,1,0:T(8,128)S(1)} %fusion.25, s32[]{:T(128)} %constant.19.clone.1), window={size=1x1x128 pad=0_0x0_0x127_0}, to_apply=%region_1.2 | reduce-window | flops 8323072 | bytes 524292 | tf_op jit(solution)/shard_map/reduce-window
  28.5 4.3 scatter_custom_fusion.1
  32.8 4.3 scatter_custom_fusion
  37.4 4.9 gather_fusion
  50.3 12.3 %all-to-all-start = ((bf16[64,18,896]{2,1,0:T(8,128)(2,1)}), bf16[64,18,896]{2,1,0:T(8,128)(2,1)}, u32[]{:S(2)}, u32[]{:S(2)}) async-start(bf16[64,18,896]{2,1,0:T(8,128)(2,1)} %broadcast_select_fusion), calls=%async_computation | async-start | bytes 5505024 | tf_op jit(solution)/shard_map/all_to_all | solution.py:39
  63.5 4.6 gather_fusion.2
  68.3 4.9 gather_fusion.3
  73.2 4.6 reshape.130
  81.8 50.9 %all-to-all-done = bf16[64,18,896]{2,1,0:T(8,128)(2,1)} async-done(((bf16[64,18,896]{2,1,0:T(8,128)(2,1)}), bf16[64,18,896]{2,1,0:T(8,128)(2,1)}, u32[]{:S(2)}, u32[]{:S(2)}) %all-to-all-start) | async-done | bytes 2064416 | tf_op jit(solution)/shard_map/all_to_all | solution.py:39
  132.8 5.7 all-to-all-start.2
  141.7 39.4 %all-gather.3.cloned.1.call-done = bf16[896,1024]{0,1:T(8,128)(2,1)} async-done(((bf16[896,16]{0,1:T(8,128)(2,1)}), bf16[896,1024]{0,1:T(8,128)(2,1)}) %all-gather.3.cloned.1.call-update) | async-done | bytes 1835024 | tf_op jit(solution)/shard_map/all_gather | solution.py:47
  188.2 5.5 convolution_convert_fusion.1
  193.6 13.7 %all-to-all-done.2 = bf16[64,18,896]{2,1,0:T(8,128)(2,1)} async-done(((bf16[64,18,896]{2,1,0:T(8,128)(2,1)}), bf16[64,18,896]{2,1,0:T(8,128)(2,1)}, u32[]{:S(2)}, u32[]{:S(2)}) %all-to-all-start.2) | async-done | bytes 2064416 | tf_op jit(solution)/shard_map/all_to_all | solution.py:73
  211.5 6.2 convolution_convert_fusion
  217.8 111.4 %all-reduce.3.cloned.1.call-done = (bf16[1152,1024]{1,0:T(8,128)(2,1)}, bf16[128,1024]{1,0:T(8,128)(2,1)}, bf16[1152,1024]{1,0:T(8,128)(2,1)}, bf16[128,1024]{1,0:T(8,128)(2,1)}) async-done(((bf16[1152,1024]{1,0:T(8,128)(2,1)}, bf16[128,1024]{1,0:T(8,128)(2,1)}, bf16[1152,1024]{1,0:T(8,128)(2,1)}, bf16[128,1024]{1,0:T(8,128)(2,1)}), (bf16[1152,1024]{1,0:T(8,128)(2,1)}, bf16[128,1024]{1,0:T(8,128)(2,1)}, ...) | async-done | bytes 5242896 | tf_op jit(solution)/shard_map/psum | solution.py:53
  346.5 10.8 %all-to-all-start.3 = ((bf16[64,18,896]{2,1,0:T(8,128)(2,1)}), bf16[64,18,896]{2,1,0:T(8,128)(2,1)}, u32[]{:S(2)}, u32[]{:S(2)}) async-start(bf16[64,18,896]{2,1,0:T(8,128)(2,1)} %reshape.127), calls=%async_computation.3 | async-start | bytes 5505024 | tf_op jit(solution)/shard_map/all_to_all | solution.py:89
  360.2 5.0 convolution_convert_fusion.3
  367.5 56.1 %all-to-all-done.3 = bf16[64,18,896]{2,1,0:T(8,128)(2,1)} async-done(((bf16[64,18,896]{2,1,0:T(8,128)(2,1)}), bf16[64,18,896]{2,1,0:T(8,128)(2,1)}, u32[]{:S(2)}, u32[]{:S(2)}) %all-to-all-start.3) | async-done | bytes 2064416 | tf_op jit(solution)/shard_map/all_to_all | solution.py:89
  423.6 7.0 %all-to-all-start.1 = ((bf16[64,18,896]{2,1,0:T(8,128)(2,1)}), bf16[64,18,896]{2,1,0:T(8,128)(2,1)}, u32[]{:S(2)}, u32[]{:S(2)}) async-start(bf16[64,18,896]{2,1,0:T(8,128)(2,1)} %reshape.124), calls=%async_computation.1 | async-start | bytes 5505024 | tf_op jit(solution)/shard_map/all_to_all | solution.py:59
  430.6 5.6 convert_bitcast_fusion.1
  443.2 5.3 gather_fusion.4
  448.5 51.4 %all-to-all-done.1 = bf16[64,18,896]{2,1,0:T(8,128)(2,1)} async-done(((bf16[64,18,896]{2,1,0:T(8,128)(2,1)}), bf16[64,18,896]{2,1,0:T(8,128)(2,1)}, u32[]{:S(2)}, u32[]{:S(2)}) %all-to-all-start.1) | async-done | bytes 2064416 | tf_op jit(solution)/shard_map/all_to_all | solution.py:59
  502.7 5.3 gather_fusion.1
  516.3 118.8 %reduce-scatter.5.cloned.1.call-done = f32[16,896]{1,0:T(8,128)} async-done(((f32[1024,896]{1,0:T(8,128)}), f32[16,896]{1,0:T(8,128)}) %reduce-scatter.5.cloned.1.call-update) | async-done | bytes 57360 | tf_op jit(solution)/shard_map/reduce_scatter | solution.py:106
  (87 shorter events, 72.9 us)
Async XLA Ops:
  7.2 181.0 %copy-start = (bf16[1,896,1024]{2,1,0:T(8,128)(2,1)S(1)}, bf16[1,896,1024]{2,1,0:T(8,128)(2,1)}, u32[]{:S(2)}) copy-start(bf16[1,896,1024]{2,1,0:T(8,128)(2,1)} %param.12) | copy-start | bytes 5505028
  7.2 30.2 %copy-start.2 = (bf16[128,896]{1,0:T(8,128)(2,1)S(1)}, bf16[128,896]{1,0:T(8,128)(2,1)}, u32[]{:S(2)}) copy-start(bf16[128,896]{1,0:T(8,128)(2,1)} %param.8) | copy-start | bytes 688132
  7.2 131.6 %all-gather.5.cloned.1.call-start = ((), (), s32[]{:S(2)}) async-start(), calls=%async_computation.7 | async-start | bytes 1863680 | tf_op jit(solution)/shard_map/all_gather | solution.py:48
  50.3 13.1 %copy-start.13 = (s32[128,8]{0,1:T(8,128)S(1)}, s32[128,8]{0,1:T(8,128)}, u32[]{:S(2)}) copy-start(s32[128,8]{0,1:T(8,128)} %param.11) | copy-start | bytes 12292
  50.3 82.5 %all-to-all-start = ((bf16[64,18,896]{2,1,0:T(8,128)(2,1)}), bf16[64,18,896]{2,1,0:T(8,128)(2,1)}, u32[]{:S(2)}, u32[]{:S(2)}) async-start(bf16[64,18,896]{2,1,0:T(8,128)(2,1)} %broadcast_select_fusion), calls=%async_computation | async-start | bytes 5505024 | tf_op jit(solution)/shard_map/all_to_all | solution.py:39
  62.6 118.5 %all-gather.3.cloned.1.call-start = ((), (), s32[]{:S(2)}) async-start(), calls=%async_computation.6 | async-start | bytes 1863680 | tf_op jit(solution)/shard_map/all_gather | solution.py:47
  63.5 4.7 copy-start.3
  132.8 74.6 %all-to-all-start.2 = ((bf16[64,18,896]{2,1,0:T(8,128)(2,1)}), bf16[64,18,896]{2,1,0:T(8,128)(2,1)}, u32[]{:S(2)}, u32[]{:S(2)}) async-start(bf16[64,18,896]{2,1,0:T(8,128)(2,1)} %select_convert_fusion), calls=%async_computation.2 | async-start | bytes 5505024 | tf_op jit(solution)/shard_map/all_to_all | solution.py:73
  138.5 190.7 %all-reduce.3.cloned.1.call-start = ((), (), s32[]{:S(2)}) async-start(), calls=%async_computation.10 | async-start | bytes 10485760 | tf_op jit(solution)/shard_map/psum | solution.py:53
  217.7 297.2 %reduce-scatter.3.cloned.1.call-start = ((), (), s32[]{:S(2)}) async-start(), calls=%async_computation.8 | async-start | bytes 3727360 | tf_op jit(solution)/shard_map/reduce_scatter | solution.py:105
  337.1 1.4 copy-start.6
  346.5 11.1 %copy-start.11 = (bf16[128,1024]{1,0:T(8,128)(2,1)S(1)}, bf16[128,1024]{1,0:T(8,128)(2,1)}, u32[]{:S(2)}) copy-start(bf16[128,1024]{1,0:T(8,128)(2,1)} %get-tuple-element.7) | copy-start | bytes 786436
  346.5 77.0 %all-to-all-start.3 = ((bf16[64,18,896]{2,1,0:T(8,128)(2,1)}), bf16[64,18,896]{2,1,0:T(8,128)(2,1)}, u32[]{:S(2)}, u32[]{:S(2)}) async-start(bf16[64,18,896]{2,1,0:T(8,128)(2,1)} %reshape.127), calls=%async_computation.3 | async-start | bytes 5505024 | tf_op jit(solution)/shard_map/all_to_all | solution.py:89
  357.3 277.8 %reduce-scatter.5.cloned.1.call-start = ((), (), s32[]{:S(2)}) async-start(), calls=%async_computation.9 | async-start | bytes 3727360 | tf_op jit(solution)/shard_map/reduce_scatter | solution.py:106
  367.5 63.1 %copy-start.7 = (bf16[1152,896]{1,0:T(8,128)(2,1)S(1)}, bf16[1152,896]{1,0:T(8,128)(2,1)}, u32[]{:S(2)}) copy-start(bf16[1152,896]{1,0:T(8,128)(2,1)} %reshape.123) | copy-start | bytes 6193156
  423.6 76.3 %all-to-all-start.1 = ((bf16[64,18,896]{2,1,0:T(8,128)(2,1)}), bf16[64,18,896]{2,1,0:T(8,128)(2,1)}, u32[]{:S(2)}, u32[]{:S(2)}) async-start(bf16[64,18,896]{2,1,0:T(8,128)(2,1)} %reshape.124), calls=%async_computation.1 | async-start | bytes 5505024 | tf_op jit(solution)/shard_map/all_to_all | solution.py:59
  430.6 5.7 copy-start.5
  430.6 5.6 copy-start.8
  508.0 2.9 copy-start.4
  508.0 4.1 copy-start.9
  512.1 1.6 copy-start.10
  512.1 1.6 copy-start.12
  512.1 124.5 %copy-start.1 = (bf16[1,896,1024]{2,1,0:T(8,128)(2,1)S(1)}, bf16[1,896,1024]{2,1,0:T(8,128)(2,1)}, u32[]{:S(2)}) copy-start(bf16[1,896,1024]{2,1,0:T(8,128)(2,1)} %param.12) | copy-start | bytes 5505028
Sparse Core Ops, SparseCore 0:
  10.7 85.2 all-gather.4
  98.7 82.3 all-gather.2
  217.8 111.2 all-reduce.2
  333.2 155.8 reduce-scatter.2
  493.6 141.5 reduce-scatter.4
where the time goes:
time: 644 us; the launch traced here: 643 us
  waiting for transfers between devices  443 us (69%)
  local copies, waits for them, and re-layouts  66.7 us (10%)
  matrix products  44.5 us (7%)
  other arithmetic  38.1 us (6%)
  starting transfers between devices  36.4 us (6%)
  between operations  14.1 us (2%)
    reduce_scatter x1, waiting for transfers between devices, local(): lax.psum_scatter(partial_out, 'expert', scatter_dimension=0, tiled=True)  119 us
    psum x1, waiting for transfers between devices, local(): lax.psum(routed_part.astype(jnp.bfloat16), 'dp').astype(jnp.float32)  111 us
    all_to_all x1, waiting for transfers between devices, local(): lax.all_to_all(input_rows.reshape(experts, capacity, features), 'expert',...  56.1 us
    all_to_all x1, waiting for transfers between devices, local(): lax.all_to_all(expert_out.reshape(experts, capacity, features), 'expert',...  51.4 us
    all_to_all x1, waiting for transfers between devices, local(): lax.all_to_all(outgoing.reshape(experts, capacity, features), 'expert', s...  50.9 us
    all_gather x1, waiting for transfers between devices, local(): lax.all_gather(shared_in, 'expert', axis=1, tiled=True)  39.4 us
    dot_general x8, matrix products, contract(): lax.dot_general(first_op, second_op, (((first_axis,), (second_axis,)), ((...  30 us
    another operation x2, other arithmetic  18 us
  transfers between devices with their start and end apart: 9, of which 7 were waited for; matrix products, arithmetic and copies ran while one was open for 21% of the time, Pallas kernels for 0%

commit v1 on v0

--- a/solution.py
+++ b/solution.py
@@ -50,7 +50,7 @@
     routed_part = jnp.dot(arrived, w_in[0], preferred_element_type=jnp.float32)
     shared_part = jnp.dot(tokens, full_in, preferred_element_type=jnp.float32)
     pre_act, shared_pre = (
-        lax.psum(routed_part.astype(jnp.bfloat16), "dp").astype(jnp.float32),
+        jnp.sum(lax.all_gather(routed_part.astype(jnp.bfloat16), "dp"), axis=0).astype(jnp.float32),
         lax.psum(shared_part.astype(jnp.bfloat16), "dp").astype(jnp.float32),
     )
     hidden = jax.nn.silu(pre_act).astype(jnp.bfloat16)

time: 644 us -> 726 us (1.13); the launches traced: 643 us -> 717 us
  waiting for transfers between devices: 443 us -> 495 us
  starting transfers between devices: 36.4 us -> 46.9 us
  other arithmetic: 38.1 us -> 47.7 us
    all_gather x0 -> x1, waiting for transfers between devices: none -> 93.6 us  [local(): lax.all_gather(routed_part.astype(jnp.bfloat16), 'dp')]
    psum x1, waiting for transfers between devices: 111 us -> 46.6 us  [local(): lax.psum(shared_part.astype(jnp.bfloat16), 'dp').astype(jnp.float32)]
    reduce_scatter x1, waiting for transfers between devices: 0.01 us -> 57.3 us  [local(): lax.psum_scatter(partial_in, 'expert', scatter_dimension=1, tiled=True)]
    all_to_all x1, waiting for transfers between devices: 56.1 us -> 0.01 us  [local(): lax.all_to_all(input_rows.reshape(experts, capacity, features), 'expert',...]
    all_to_all x1, waiting for transfers between devices: 13.7 us -> 55 us  [local(): lax.all_to_all(grad_out.reshape(experts, capacity, features), 'expert', s...]
    all_gather x1, waiting for transfers between devices: 39.4 us -> 0.02 us  [local(): lax.all_gather(shared_in, 'expert', axis=1, tiled=True)]
    all_gather x1, waiting for transfers between devices: 0.02 us -> 35.1 us  [local(): lax.all_gather(shared_out, 'expert', axis=0, tiled=True)]
    all_to_all x1, waiting for transfers between devices: 50.9 us -> 17.7 us  [local(): lax.all_to_all(outgoing.reshape(experts, capacity, features), 'expert', s...]
  transfers between devices with their start and end apart: 9 -> 10, of which waited for: 7 -> 8; matrix products, arithmetic and copies ran while one was open for 21% -> 20% of each run, Pallas kernels for 0% -> 0%
where the time goes in v1:
time: 726 us; the launch traced here: 717 us
  waiting for transfers between devices  495 us (68%)
  local copies, waits for them, and re-layouts  66.2 us (9%)
  other arithmetic  47.7 us (7%)
  starting transfers between devices  46.9 us (6%)
  matrix products  46.6 us (6%)
  between operations  14.4 us (2%)
    reduce_scatter x1, waiting for transfers between devices, local(): lax.psum_scatter(partial_out, 'expert', scatter_dimension=0, tiled=True)  145 us
    all_gather x1, waiting for transfers between devices, local(): lax.all_gather(routed_part.astype(jnp.bfloat16), 'dp')  93.6 us
    reduce_scatter x1, waiting for transfers between devices, local(): lax.psum_scatter(partial_in, 'expert', scatter_dimension=1, tiled=True)  57.3 us
    all_to_all x1, waiting for transfers between devices, local(): lax.all_to_all(grad_out.reshape(experts, capacity, features), 'expert', s...  55 us
    psum x1, waiting for transfers between devices, local(): lax.psum(shared_part.astype(jnp.bfloat16), 'dp').astype(jnp.float32)  46.6 us
    all_to_all x1, waiting for transfers between devices, local(): lax.all_to_all(expert_out.reshape(experts, capacity, features), 'expert',...  43 us
    all_gather x1, waiting for transfers between devices, local(): lax.all_gather(shared_out, 'expert', axis=0, tiled=True)  35.1 us
    dot_general x8, matrix products, contract(): lax.dot_general(first_op, second_op, (((first_axis,), (second_axis,)), ((...  29 us
  transfers between devices with their start and end apart: 10, of which 8 were waited for; matrix products, arithmetic and copies ran while one was open for 20% of the time, Pallas kernels for 0%

profile of v1, /device:TPU:8, one launch (start us, length us, event | category | flops | bytes accessed | tf_op | source)
XLA Modules:
  0.0 716.9 jit_solution(9923323817819807015)
XLA Ops:
  9.8 18.0 %reduce-window.6 = s32[64,8,128]{2,1,0:T(8,128)S(1)} reduce-window(s32[64,8,128]{2,1,0:T(8,128)S(1)} %fusion.25, s32[]{:T(128)} %constant.22.clone.1), window={size=1x1x128 pad=0_0x0_0x127_0}, to_apply=%region_1.2 | reduce-window | flops 8323072 | bytes 524292 | tf_op jit(solution)/shard_map/reduce-window
  37.5 4.9 gather_fusion.3
  47.0 4.6 gather_fusion.2
  55.8 12.3 %all-to-all-start.2 = ((bf16[64,18,896]{2,1,0:T(8,128)(2,1)}), bf16[64,18,896]{2,1,0:T(8,128)(2,1)}, u32[]{:S(2)}, u32[]{:S(2)}) async-start(bf16[64,18,896]{2,1,0:T(8,128)(2,1)} %select_convert_fusion), calls=%async_computation.2 | async-start | bytes 5505024 | tf_op jit(solution)/shard_map/all_to_all | solution.py:73
  68.8 4.9 gather_fusion
  81.7 55.0 %all-to-all-done.2 = bf16[64,18,896]{2,1,0:T(8,128)(2,1)} async-done(((bf16[64,18,896]{2,1,0:T(8,128)(2,1)}), bf16[64,18,896]{2,1,0:T(8,128)(2,1)}, u32[]{:S(2)}, u32[]{:S(2)}) %all-to-all-start.2) | async-done | bytes 2064416 | tf_op jit(solution)/shard_map/all_to_all | solution.py:73
  136.7 6.5 all-to-all-start
  146.5 35.1 %all-gather.7.cloned.1.call-done = bf16[1024,896]{1,0:T(8,128)(2,1)} async-done(((bf16[16,896]{1,0:T(8,128)(2,1)}), bf16[1024,896]{1,0:T(8,128)(2,1)}) %all-gather.7.cloned.1.call-update) | async-done | bytes 1835024 | tf_op jit(solution)/shard_map/all_gather | solution.py:48
  188.8 5.5 convolution_convert_fusion
  194.3 17.7 %all-to-all-done = bf16[64,18,896]{2,1,0:T(8,128)(2,1)} async-done(((bf16[64,18,896]{2,1,0:T(8,128)(2,1)}), bf16[64,18,896]{2,1,0:T(8,128)(2,1)}, u32[]{:S(2)}, u32[]{:S(2)}) %all-to-all-start) | async-done | bytes 2064416 | tf_op jit(solution)/shard_map/all_to_all | solution.py:39
  216.2 6.2 convolution_convert_fusion.1
  222.5 46.6 %all-reduce.3.cloned.1.call-done = (bf16[128,1024]{1,0:T(8,128)(2,1)}, bf16[1152,1024]{1,0:T(8,128)(2,1)}, bf16[128,1024]{1,0:T(8,128)(2,1)}) async-done(((bf16[128,1024]{1,0:T(8,128)(2,1)}, bf16[1152,1024]{1,0:T(8,128)(2,1)}, bf16[128,1024]{1,0:T(8,128)(2,1)}), (bf16[128,1024]{1,0:T(8,128)(2,1)}, bf16[1152,1024]{1,0:T(8,128)(2,1)}, bf16[128,1024]{1,0:T(8,128)(2,1)})) %all-reduce.3.cloned.1.call-update) | async-done | bytes 2883600 | tf_op jit(solution)/shard_map/psum | solution.py:54
  272.8 93.6 %all-gather.9.cloned.1.call-done = bf16[4608,1024]{1,0:T(8,128)(2,1)} async-done(((bf16[1152,1024]{1,0:T(8,128)(2,1)}), bf16[4608,1024]{1,0:T(8,128)(2,1)}) %all-gather.9.cloned.1.call-update) | async-done | bytes 9437200 | tf_op jit(solution)/shard_map/all_gather | solution.py:53
  366.3 8.2 %reduce_sum.43 = bf16[1152,1024]{1,0:T(8,128)(2,1)} reduce(bf16[4,1152,1024]{2,1,0:T(8,128)(2,1)} %bitcast.53, bf16[]{:T(256)} %constant.48.clone.1), dimensions={0}, to_apply=%region_6.7 | reduce | flops 3538944 | bytes 11796482 | tf_op jit(solution)/shard_map/reduce_sum | solution.py:53
  374.5 5.7 convolution_convert_fusion.3
  384.4 10.8 %all-to-all-start.1 = ((bf16[64,18,896]{2,1,0:T(8,128)(2,1)}), bf16[64,18,896]{2,1,0:T(8,128)(2,1)}, u32[]{:S(2)}, u32[]{:S(2)}) async-start(bf16[64,18,896]{2,1,0:T(8,128)(2,1)} %reshape.124), calls=%async_computation.1 | async-start | bytes 5505024 | tf_op jit(solution)/shard_map/all_to_all | solution.py:59
  395.2 9.6 %reduce-scatter.5.cloned.1.call-start = ((), (), s32[]{:S(2)}) async-start(), calls=%async_computation.9 | async-start | bytes 3727360 | tf_op jit(solution)/shard_map/reduce_scatter | solution.py:106
  418.4 43.0 %all-to-all-done.1 = bf16[64,18,896]{2,1,0:T(8,128)(2,1)} async-done(((bf16[64,18,896]{2,1,0:T(8,128)(2,1)}), bf16[64,18,896]{2,1,0:T(8,128)(2,1)}, u32[]{:S(2)}, u32[]{:S(2)}) %all-to-all-start.1) | async-done | bytes 2064416 | tf_op jit(solution)/shard_map/all_to_all | solution.py:59
  461.4 7.1 all-to-all-start.3
  468.6 57.3 %reduce-scatter.3.cloned.1.call-done = f32[896,16]{0,1:T(8,128)} async-done(((f32[896,1024]{0,1:T(8,128)}), f32[896,16]{0,1:T(8,128)}) %reduce-scatter.3.cloned.1.call-update) | async-done | bytes 57360 | tf_op jit(solution)/shard_map/reduce_scatter | solution.py:105
  527.4 145.2 %reduce-scatter.5.cloned.1.call-done = f32[16,896]{1,0:T(8,128)} async-done(((f32[1024,896]{1,0:T(8,128)}), f32[16,896]{1,0:T(8,128)}) %reduce-scatter.5.cloned.1.call-update) | async-done | bytes 57360 | tf_op jit(solution)/shard_map/reduce_scatter | solution.py:106
  674.0 6.2 convert_bitcast_fusion.1
  687.2 5.3 gather_fusion.1
  697.9 5.3 gather_fusion.4
  (87 shorter events, 87.8 us)
Async XLA Ops:
  7.2 181.6 %copy-start = (bf16[1,1024,896]{2,1,0:T(8,128)(2,1)S(1)}, bf16[1,1024,896]{2,1,0:T(8,128)(2,1)}, u32[]{:S(2)}) copy-start(bf16[1,1024,896]{2,1,0:T(8,128)(2,1)} %param.13) | copy-start | bytes 5505028
  7.2 30.1 %copy-start.10 = (s32[128,8]{0,1:T(8,128)S(1)}, s32[128,8]{0,1:T(8,128)}, u32[]{:S(2)}) copy-start(s32[128,8]{0,1:T(8,128)} %param.11) | copy-start | bytes 12292
  7.2 30.3 %copy-start.3 = (bf16[128,896]{1,0:T(8,128)(2,1)S(1)}, bf16[128,896]{1,0:T(8,128)(2,1)}, u32[]{:S(2)}) copy-start(bf16[128,896]{1,0:T(8,128)(2,1)} %param.9) | copy-start | bytes 688132
  7.2 136.4 %all-gather.5.cloned.1.call-start = ((), (), s32[]{:S(2)}) async-start(), calls=%async_computation.6 | async-start | bytes 1863680 | tf_op jit(solution)/shard_map/all_gather | solution.py:47
  55.8 13.1 %copy-start.2 = (bf16[128,896]{1,0:T(8,128)(2,1)S(1)}, bf16[128,896]{1,0:T(8,128)(2,1)}, u32[]{:S(2)}) copy-start(bf16[128,896]{1,0:T(8,128)(2,1)} %param.8) | copy-start | bytes 688132
  55.8 80.9 %all-to-all-start.2 = ((bf16[64,18,896]{2,1,0:T(8,128)(2,1)}), bf16[64,18,896]{2,1,0:T(8,128)(2,1)}, u32[]{:S(2)}, u32[]{:S(2)}) async-start(bf16[64,18,896]{2,1,0:T(8,128)(2,1)} %select_convert_fusion), calls=%async_computation.2 | async-start | bytes 5505024 | tf_op jit(solution)/shard_map/all_to_all | solution.py:73
  68.1 113.6 %all-gather.7.cloned.1.call-start = ((), (), s32[]{:S(2)}) async-start(), calls=%async_computation.7 | async-start | bytes 1863680 | tf_op jit(solution)/shard_map/all_gather | solution.py:48
  136.7 75.4 %all-to-all-start = ((bf16[64,18,896]{2,1,0:T(8,128)(2,1)}), bf16[64,18,896]{2,1,0:T(8,128)(2,1)}, u32[]{:S(2)}, u32[]{:S(2)}) async-start(bf16[64,18,896]{2,1,0:T(8,128)(2,1)} %broadcast_select_fusion), calls=%async_computation | async-start | bytes 5505024 | tf_op jit(solution)/shard_map/all_to_all | solution.py:39
  143.2 125.9 %all-reduce.3.cloned.1.call-start = ((), (), s32[]{:S(2)}) async-start(), calls=%async_computation.11 | async-start | bytes 5767168 | tf_op jit(solution)/shard_map/psum | solution.py:54
  194.3 172.1 %all-gather.9.cloned.1.call-start = ((), (), s32[]{:S(2)}) async-start(), calls=%async_computation.10 | async-start | bytes 11796480 | tf_op jit(solution)/shard_map/all_gather | solution.py:53
  222.4 303.5 %reduce-scatter.3.cloned.1.call-start = ((), (), s32[]{:S(2)}) async-start(), calls=%async_computation.8 | async-start | bytes 3727360 | tf_op jit(solution)/shard_map/reduce_scatter | solution.py:105
  384.4 20.4 %copy-start.8 = (bf16[128,1024]{1,0:T(8,128)(2,1)S(1)}, bf16[128,1024]{1,0:T(8,128)(2,1)}, u32[]{:S(2)}) copy-start(bf16[128,1024]{1,0:T(8,128)(2,1)} %get-tuple-element.6) | copy-start | bytes 786436
  384.4 77.1 %all-to-all-start.1 = ((bf16[64,18,896]{2,1,0:T(8,128)(2,1)}), bf16[64,18,896]{2,1,0:T(8,128)(2,1)}, u32[]{:S(2)}, u32[]{:S(2)}) async-start(bf16[64,18,896]{2,1,0:T(8,128)(2,1)} %reshape.124), calls=%async_computation.1 | async-start | bytes 5505024 | tf_op jit(solution)/shard_map/all_to_all | solution.py:59
  395.2 277.4 %reduce-scatter.5.cloned.1.call-start = ((), (), s32[]{:S(2)}) async-start(), calls=%async_computation.9 | async-start | bytes 3727360 | tf_op jit(solution)/shard_map/reduce_scatter | solution.py:106
  407.3 5.9 copy-start.11
  411.8 1.4 copy-start.5
  461.4 233.7 %all-to-all-start.3 = ((bf16[64,18,896]{2,1,0:T(8,128)(2,1)}), bf16[64,18,896]{2,1,0:T(8,128)(2,1)}, u32[]{:S(2)}, u32[]{:S(2)}) async-start(bf16[64,18,896]{2,1,0:T(8,128)(2,1)} %reshape.127), calls=%async_computation.3 | async-start | bytes 5505024 | tf_op jit(solution)/shard_map/all_to_all | solution.py:89
  674.0 6.2 copy-start.4
  674.0 6.2 copy-start.6
  705.9 2.9 copy-start.7
  706.0 2.8 copy-start.9
  706.0 4.1 copy-start.1
Sparse Core Ops, SparseCore 0:
  10.7 83.0 all-gather.4
  96.6 85.0 all-gather.6
  194.4 74.6 all-reduce.2
  270.8 95.5 all-gather.8
  370.3 155.5 reduce-scatter.2
  530.5 142.0 reduce-scatter.4
